TPU v7x, 512 devices: a whole 4x8x8 slice. The times are simulated.
512 devices in a mesh: sta: 128 (over z_hi, y, x, core), cell: 4 (over z_lo).
Axes of the slice: x: 4, y: 8, z: 8 (z_hi: 2, z_lo: 4; z = z_hi * 4 + z_lo), core: 2. Of those that a mesh axis runs over, the one named last changes fastest.
Arguments:
- sensitivity: bfloat16 [2048, 52, 2048], P('sta', None, 'cell'), may hold values from -0.01953125 to 0.01953125
- footprint: int32 [128, 52], P('sta'), may hold values from 0 to 63, as said below
- linked: int32 [128, 9], P('sta'), may hold values from 0 to 1, as said below
- smooth_x: bfloat16 [16, 16], replicated, may hold values from 0 to 8, as said below
- smooth_y: bfloat16 [64, 64], replicated, may hold values from 0 to 8, as said below
- smooth_z: bfloat16 [128, 128], replicated, may hold values from 0 to 8, as said below
Outputs:
- band: float32 [2048, 144], P('sta', 'cell')
Inputs may be any that keep to these rules, and one draw needn't show every extreme that they name: `footprint`: within a row the 52 tiles are different. linked[b, 4] is 1, and linked[b, 4 + k] equals linked[(b + k) mod the number of row blocks, 4 - k] for 1 <= k <= 4. `smooth_x`: Symmetric, with positive entries. `smooth_y`: Symmetric, with positive entries. `smooth_z`: Symmetric, with positive entries.
All inputs are finite; a program needn't handle non-finite values.
Results may differ from a plain program's by a relative error of at most 0.005.
Values may be sent and summed in bfloat16 or wider, within the bound.
A program may use at most 64 MiB of HBM per device.

v0:
```python
import math

import jax
import jax.numpy as jnp
from jax import lax
from jax.sharding import PartitionSpec as P

TILE = 16
HALF = 4
TILES = 64
BAND = 9


def from_behind(block, axis, distance):
    devices = range(lax.axis_size(axis))
    route = [((i - distance) % len(devices), i) for i in devices]
    return lax.ppermute(block, axis, route)


def in_blocks(array, dim, size):
    before, after = (array.shape[:dim], array.shape[dim + 1 :])
    return jnp.moveaxis(array.reshape(*before, size, -1, *after), dim, 0)


def sent_and_summed(array, axis, dim):
    blocks = in_blocks(array, dim, lax.axis_size(axis))
    arrived = lax.all_to_all(blocks, axis, split_axis=0, concat_axis=0, tiled=True)
    return arrived.sum(axis=0)


def spread_tiles(values, foot_tiles):
    onehot = (foot_tiles[:, None] == jnp.arange(TILES, dtype=jnp.int32)[None, :]).astype(
        jnp.bfloat16
    )
    placed = jnp.einsum("rfk,ft->rtk", values, onehot, preferred_element_type=jnp.float32)
    return placed.astype(jnp.bfloat16)


def smooth_depth(block, smooth_z):
    row_count, tile_count, slab_width = block.shape
    depth_cells = smooth_z.shape[0]
    grid_field = block.reshape(row_count, tile_count, depth_cells, slab_width // depth_cells)
    smoothed = jnp.einsum("rtzc,wz->rtwc", grid_field, smooth_z, preferred_element_type=jnp.float32)
    return smoothed.astype(jnp.bfloat16).reshape(row_count, tile_count, slab_width)


def smooth_plane(field_rows, smooth_x, smooth_y):
    row_count, tile_count, slab_width = field_rows.shape
    cells_across = smooth_x.shape[0]
    blocks_along = tile_count // cells_across
    group_rows = math.gcd(row_count, 4)
    y_kernel = smooth_y.reshape(blocks_along, TILE, blocks_along, TILE)

    def smooth_group(row_group):
        grid_field = row_group.reshape(
            group_rows, cells_across, blocks_along, slab_width // TILE, TILE
        )
        across = jnp.einsum(
            "rxbzc,vx->rvbzc", grid_field, smooth_x, preferred_element_type=jnp.float32
        ).astype(jnp.bfloat16)
        along = jnp.einsum(
            "rxbzc,ekbc->rxezk", across, y_kernel, preferred_element_type=jnp.float32
        ).astype(jnp.bfloat16)
        return along.reshape(group_rows, tile_count, slab_width)

    grouped = field_rows.reshape(row_count // group_rows, group_rows, tile_count, slab_width)
    return lax.map(smooth_group, grouped).reshape(row_count, tile_count, slab_width)


def pair_tile(smoothed, values, foot_tiles):
    row_count = smoothed.shape[0]
    picked = jnp.take(smoothed, foot_tiles, axis=1).reshape(row_count, -1)
    partner = values.reshape(values.shape[0], -1)
    return lax.dot_general(
        picked, partner, (((1,), (1,)), ((), ())), preferred_element_type=jnp.float32
    )


def body(sensitivity, footprint, linked, smooth_x, smooth_y, smooth_z):
    own_tiles = footprint[0]
    depth_rows = lax.all_to_all(
        smooth_depth(
            lax.all_to_all(sensitivity, "cell", split_axis=1, concat_axis=2, tiled=True), smooth_z
        ),
        "cell",
        split_axis=2,
        concat_axis=1,
        tiled=True,
    )
    grid_rows = spread_tiles(depth_rows, own_tiles)
    smoothed = smooth_plane(grid_rows, smooth_x, smooth_y)
    pair_flags = linked[0]

    def masked_tile(values, foot_tiles, flag):
        return pair_tile(smoothed, values, foot_tiles) * flag.astype(jnp.float32)

    band_parts = [None] * BAND
    band_parts[HALF] = masked_tile(sensitivity, own_tiles, pair_flags[HALF])
    carried = (sensitivity, footprint)
    for offset in range(1, HALF + 1):
        carried = from_behind((carried[0], carried[1]), "sta", 1)
        band_parts[HALF - offset] = masked_tile(
            carried[0], carried[1][0], pair_flags[HALF - offset]
        )
    for offset in range(1, HALF + 1):
        band_parts[HALF + offset] = from_behind(band_parts[HALF - offset].T, "sta", -offset)
    partial_band = jnp.concatenate(band_parts, axis=1)
    return sent_and_summed(partial_band, "cell", 1)


def solution(mesh):
    return jax.shard_map(
        body,
        mesh=mesh,
        in_specs=(P("sta", None, "cell"), P("sta", None), P("sta", None), P(), P(), P()),
        out_specs=P("sta", "cell"),
        check_vma=False,
    )
```

profile of v0, /device:TPU:62, one launch (start us, length us, event | category | flops | bytes accessed | tf_op | source)
XLA Modules:
  0.0 227.8 jit_solution(7614213136167638222)
XLA Ops:
  0.0 7.4 %all-to-all-start = ((bf16[16,52,512]{2,0,1:T(8,128)(2,1)}), bf16[16,52,512]{2,0,1:T(8,128)(2,1)S(1)}, u32[]{:S(2)}, u32[]{:S(2)}) async-start(bf16[16,52,512]{2,0,1:T(8,128)(2,1)} %param.10), calls=%async_computation | async-start | bytes 1703936 | tf_op jit(solution)/shard_map/all_to_all | solution.py:83
  9.3 7.4 %collective-permute-start = (s32[1,52]{1,0:T(1,128)}, s32[1,52]{1,0:T(1,128)S(1)}, u32[]{:S(2)}, u32[]{:S(2)}) collective-permute-start(s32[1,52]{1,0:T(1,128)} %param.11), channel_id=1, source_target_pairs={{508,0},{0,4},{4,8},{8,12},{12,16},{16,20},{20,24},{24,28},{28,32}... | collective-permute-start | bytes 632 | tf_op jit(solution)/shard_map/ppermute | solution.py:17
  23.5 9.2 %collective-permute-start.1 = (s32[1,52]{1,0:T(1,128)S(1)}, s32[1,52]{1,0:T(1,128)S(1)}, u32[]{:S(2)}, u32[]{:S(2)}) collective-permute-start(s32[1,52]{1,0:T(1,128)S(1)} %collective-permute-done), channel_id=1, source_target_pairs={{508,0},{0,4},{4,8},{8,12},{12,16},{16,20},{20,24},{24,28},{28,32}... | collective-permute-start | bytes 632 | tf_op jit(solution)/shard_map/ppermute | solution.py:17
  33.5 15.7 %collective-permute-start.2 = (s32[1,52]{1,0:T(1,128)S(1)}, s32[1,52]{1,0:T(1,128)S(1)}, u32[]{:S(2)}, u32[]{:S(2)}) collective-permute-start(s32[1,52]{1,0:T(1,128)S(1)} %collective-permute-done.1), channel_id=1, source_target_pairs={{508,0},{0,4},{4,8},{8,12},{12,16},{16,20},{20,24},{24,28},{28,32}... | collective-permute-start | bytes 632 | tf_op jit(solution)/shard_map/ppermute | solution.py:17
  49.2 12.3 %collective-permute-start.5 = (bf16[16,52,512]{2,0,1:T(8,128)(2,1)S(1)}, bf16[16,52,512]{2,0,1:T(8,128)(2,1)}, u32[]{:S(2)}, u32[]{:S(2)}) collective-permute-start(bf16[16,52,512]{2,0,1:T(8,128)(2,1)S(1)} %collective-permute-done.4), channel_id=1, source_target_pairs={{508,0},{0,4},{4,8},{8,12},{12,16},{16,20},{20,24},{24,28},{28,32}... | collective-permute-start | bytes 2555912 | tf_op jit(solution)/shard_map/ppermute | solution.py:17
  62.2 6.1 %reshape.56 = bf16[16,13,128,16]{3,2,1,0:T(8,128)(2,1)} reshape(bf16[16,13,4,512]{3,2,1,0:T(4,128)(2,1)S(1)} %bitcast.140) | data formatting | bytes 1703936 | tf_op jit(solution)/shard_map/reshape | solution.py:42
  68.3 4.8 %fusion.5 = bf16[16,13,128,16]{2,3,1,0:T(8,128)(2,1)S(1)} fusion(bf16[16,13,128,16]{3,2,1,0:T(8,128)(2,1)} %reshape.56, bf16[128,128]{1,0:T(8,128)(2,1)S(1)} %copy-done), kind=kOutput, calls=%fused_computation.16 | convolution fusion | flops 109477888 | bytes 1736704 | tf_op jit(solution)/shard_map/rtzc,wz->rtwc/dot_general | solution.py:43
  73.2 12.5 %copy.60 = bf16[16,13,128,16]{0,1,3,2:T(8,128)(2,1)} copy(bf16[16,13,128,16]{2,3,1,0:T(8,128)(2,1)S(1)} %fusion.5) | data formatting | bytes 1703936 | tf_op jit(solution)/shard_map/reshape | solution.py:44
  85.7 8.3 %reshape.128 = bf16[4,2,53248]{2,1,0:T(2,128)(2,1)} reshape(bf16[2048,13,16]{2,1,0:T(8,128)(2,1)} %bitcast.135) | data formatting | bytes 1703936
  94.0 5.8 %all-to-all-start.1 = ((bf16[4,2,53248]{2,1,0:T(2,128)(2,1)}), bf16[4,2,53248]{2,1,0:T(2,128)(2,1)S(1)}, u32[]{:S(2)}, u32[]{:S(2)}) async-start(bf16[4,2,53248]{2,1,0:T(2,128)(2,1)} %reshape.128), calls=%async_computation.1 | async-start | bytes 1703936 | tf_op jit(solution)/shard_map/all_to_all | solution.py:81
  101.8 2.1 collective-permute-start.6
  104.8 16.7 %all-to-all-done.1 = bf16[4,2,53248]{2,1,0:T(2,128)(2,1)S(1)} async-done(((bf16[4,2,53248]{2,1,0:T(2,128)(2,1)}), bf16[4,2,53248]{2,1,0:T(2,128)(2,1)S(1)}, u32[]{:S(2)}, u32[]{:S(2)}) %all-to-all-start.1) | async-done | bytes 852000 | tf_op jit(solution)/shard_map/all_to_all | solution.py:81
  121.5 7.7 %reshape.129 = bf16[2048,13,16]{2,1,0:T(8,128)(2,1)} reshape(bf16[4,2,53248]{2,1,0:T(2,128)(2,1)S(1)} %all-to-all-done.1) | data formatting | bytes 1703936
  129.3 9.3 %copy.61 = bf16[16,13,4,512]{3,2,0,1:T(4,128)(2,1)S(1)} copy(bf16[16,13,4,512]{0,1,3,2:T(8,128)(2,1)} %bitcast.136) | data formatting | bytes 1703936 | tf_op jit(solution)/shard_map/all_to_all | solution.py:81
  138.8 2.3 convolution_convert_fusion.1
  143.0 40.5 %while.10 = (s32[]{:T(128)}, bf16[4,4,64,512]{3,2,1,0:T(8,128)(2,1)}, bf16[4,4,64,512]{3,2,1,0:T(8,128)(2,1)}, bf16[16,16]{1,0:T(8,128)(2,1)S(1)}, bf16[4,16,4,16]{3,1,2,0:T(8,128)(2,1)S(1)}, /*index=5*/s32[]{:T(128)}) while((s32[]{:T(128)}, bf16[4,4,64,512]{3,2,1,0:T(8,128)(2,1)}, bf16[4,4,64,512]{3,2,1,0:T(8,128)(2,1)}, ...), condition=%wide.region_1.2_spmd, body=%wide.region_0.1_spmd.sunk | while | flops 21233664 | bytes 4203593 | solution.py:67
  148.8 3.6 %broadcast_in_dim.31 = bf16[1,4,64,512]{3,2,1,0:T(8,128)(2,1)S(1)} reshape(bf16[4,16,4,32,16]{4,3,2,1,0:T(8,128)(2,1)S(1)} %copy.80) | data formatting | bytes 524288 | tf_op jit(solution)/shard_map/while/body/jit(dynamic_update_index_in_dim)/broadcast_in_dim | solution.py:67
  158.9 3.6 %broadcast_in_dim.31 = bf16[1,4,64,512]{3,2,1,0:T(8,128)(2,1)S(1)} reshape(bf16[4,16,4,32,16]{4,3,2,1,0:T(8,128)(2,1)S(1)} %copy.80) | data formatting | bytes 524288 | tf_op jit(solution)/shard_map/while/body/jit(dynamic_update_index_in_dim)/broadcast_in_dim | solution.py:67
  169.0 3.6 %broadcast_in_dim.31 = bf16[1,4,64,512]{3,2,1,0:T(8,128)(2,1)S(1)} reshape(bf16[4,16,4,32,16]{4,3,2,1,0:T(8,128)(2,1)S(1)} %copy.80) | data formatting | bytes 524288 | tf_op jit(solution)/shard_map/while/body/jit(dynamic_update_index_in_dim)/broadcast_in_dim | solution.py:67
  179.2 3.6 %broadcast_in_dim.31 = bf16[1,4,64,512]{3,2,1,0:T(8,128)(2,1)S(1)} reshape(bf16[4,16,4,32,16]{4,3,2,1,0:T(8,128)(2,1)S(1)} %copy.80) | data formatting | bytes 524288 | tf_op jit(solution)/shard_map/while/body/jit(dynamic_update_index_in_dim)/broadcast_in_dim | solution.py:67
  196.8 3.7 %collective-permute-start.8 = (f32[16,16]{1,0:T(8,128)S(1)}, f32[16,16]{1,0:T(8,128)S(1)}, u32[]{:S(2)}, u32[]{:S(2)}) collective-permute-start(f32[16,16]{1,0:T(8,128)S(1)} %bitcast.145), channel_id=1, source_target_pairs={{4,0},{8,4},{12,8},{16,12},{20,16},{24,20},{28,24},{32,28},{36,32}... | collective-permute-start | bytes 3080 | tf_op jit(solution)/shard_map/ppermute | solution.py:17
  202.9 1.9 collective-permute-start.11
  207.4 10.1 %collective-permute-done.11 = f32[16,16]{1,0:T(8,128)S(1)} collective-permute-done((f32[16,16]{1,0:T(8,128)S(1)}, f32[16,16]{1,0:T(8,128)S(1)}, u32[]{:S(2)}, u32[]{:S(2)}) %collective-permute-start.11) | collective-permute-done | bytes 1056 | tf_op jit(solution)/shard_map/ppermute | solution.py:17
  217.8 8.1 %all_to_all.38 = f32[4,1,576]{2,1,0:T(1,128)S(1)} all-to-all(f32[4,1,576]{2,1,0:T(1,128)S(1)} %reshape.130), channel_id=1, replica_groups=mesh['sta'=128,'cell'=4] {'cell'}, dimensions={0} | all-to-all | bytes 18432 | tf_op jit(solution)/shard_map/all_to_all | solution.py:27
  (97 shorter events, 58.2 us)
Async XLA Ops:
  0.0 68.3 %copy-start = (bf16[128,128]{1,0:T(8,128)(2,1)S(1)}, bf16[128,128]{1,0:T(8,128)(2,1)}, u32[]{:S(2)}) copy-start(bf16[128,128]{1,0:T(8,128)(2,1)} %param.15) | copy-start | bytes 98308
  0.0 61.5 %all-to-all-start = ((bf16[16,52,512]{2,0,1:T(8,128)(2,1)}), bf16[16,52,512]{2,0,1:T(8,128)(2,1)S(1)}, u32[]{:S(2)}, u32[]{:S(2)}) async-start(bf16[16,52,512]{2,0,1:T(8,128)(2,1)} %param.10), calls=%async_computation | async-start | bytes 1703936 | tf_op jit(solution)/shard_map/all_to_all | solution.py:83
  7.4 41.8 %collective-permute-start.4 = (bf16[16,52,512]{2,0,1:T(8,128)(2,1)}, bf16[16,52,512]{2,0,1:T(8,128)(2,1)S(1)}, u32[]{:S(2)}, u32[]{:S(2)}) collective-permute-start(bf16[16,52,512]{2,0,1:T(8,128)(2,1)} %param.10), channel_id=1, source_target_pairs={{508,0},{0,4},{4,8},{8,12},{12,16},{16,20},{20,24},{24,28},{28,32}... | collective-permute-start | bytes 2555912 | tf_op jit(solution)/shard_map/ppermute | solution.py:17
  9.3 14.2 %collective-permute-start = (s32[1,52]{1,0:T(1,128)}, s32[1,52]{1,0:T(1,128)S(1)}, u32[]{:S(2)}, u32[]{:S(2)}) collective-permute-start(s32[1,52]{1,0:T(1,128)} %param.11), channel_id=1, source_target_pairs={{508,0},{0,4},{4,8},{8,12},{12,16},{16,20},{20,24},{24,28},{28,32}... | collective-permute-start | bytes 632 | tf_op jit(solution)/shard_map/ppermute | solution.py:17
  23.5 10.0 %collective-permute-start.1 = (s32[1,52]{1,0:T(1,128)S(1)}, s32[1,52]{1,0:T(1,128)S(1)}, u32[]{:S(2)}, u32[]{:S(2)}) collective-permute-start(s32[1,52]{1,0:T(1,128)S(1)} %collective-permute-done), channel_id=1, source_target_pairs={{508,0},{0,4},{4,8},{8,12},{12,16},{16,20},{20,24},{24,28},{28,32}... | collective-permute-start | bytes 632 | tf_op jit(solution)/shard_map/ppermute | solution.py:17
  33.5 66.4 %collective-permute-start.2 = (s32[1,52]{1,0:T(1,128)S(1)}, s32[1,52]{1,0:T(1,128)S(1)}, u32[]{:S(2)}, u32[]{:S(2)}) collective-permute-start(s32[1,52]{1,0:T(1,128)S(1)} %collective-permute-done.1), channel_id=1, source_target_pairs={{508,0},{0,4},{4,8},{8,12},{12,16},{16,20},{20,24},{24,28},{28,32}... | collective-permute-start | bytes 632 | tf_op jit(solution)/shard_map/ppermute | solution.py:17
  49.2 24.0 %copy-start.3 = (bf16[16,52,512]{2,0,1:T(8,128)(2,1)}, bf16[16,52,512]{2,0,1:T(8,128)(2,1)S(1)}, u32[]{:S(2)}) copy-start(bf16[16,52,512]{2,0,1:T(8,128)(2,1)S(1)} %collective-permute-done.4) | copy-start | bytes 2555908
  49.2 52.6 %collective-permute-start.5 = (bf16[16,52,512]{2,0,1:T(8,128)(2,1)S(1)}, bf16[16,52,512]{2,0,1:T(8,128)(2,1)}, u32[]{:S(2)}, u32[]{:S(2)}) collective-permute-start(bf16[16,52,512]{2,0,1:T(8,128)(2,1)S(1)} %collective-permute-done.4), channel_id=1, source_target_pairs={{508,0},{0,4},{4,8},{8,12},{12,16},{16,20},{20,24},{24,28},{28,32}... | collective-permute-start | bytes 2555912 | tf_op jit(solution)/shard_map/ppermute | solution.py:17
  94.0 27.5 %all-to-all-start.1 = ((bf16[4,2,53248]{2,1,0:T(2,128)(2,1)}), bf16[4,2,53248]{2,1,0:T(2,128)(2,1)S(1)}, u32[]{:S(2)}, u32[]{:S(2)}) async-start(bf16[4,2,53248]{2,1,0:T(2,128)(2,1)} %reshape.128), calls=%async_computation.1 | async-start | bytes 1703936 | tf_op jit(solution)/shard_map/all_to_all | solution.py:81
  99.9 4.9 %collective-permute-start.3 = (s32[1,52]{1,0:T(1,128)S(1)}, s32[1,52]{1,0:T(1,128)S(1)}, u32[]{:S(2)}, u32[]{:S(2)}) collective-permute-start(s32[1,52]{1,0:T(1,128)S(1)} %collective-permute-done.2), channel_id=1, source_target_pairs={{508,0},{0,4},{4,8},{8,12},{12,16},{16,20},{20,24},{24,28},{28,32}... | collective-permute-start | bytes 632 | tf_op jit(solution)/shard_map/ppermute | solution.py:17
  101.8 39.2 %collective-permute-start.6 = (bf16[16,52,512]{2,0,1:T(8,128)(2,1)}, bf16[16,52,512]{2,0,1:T(8,128)(2,1)}, u32[]{:S(2)}, u32[]{:S(2)}) collective-permute-start(bf16[16,52,512]{2,0,1:T(8,128)(2,1)} %collective-permute-done.5), channel_id=1, source_target_pairs={{508,0},{0,4},{4,8},{8,12},{12,16},{16,20},{20,24},{24,28},{28,32}... | collective-permute-start | bytes 2555912 | tf_op jit(solution)/shard_map/ppermute | solution.py:17
  129.3 9.5 %copy-start.2 = (s32[1,52]{1,0:T(1,128)S(1)}, s32[1,52]{1,0:T(1,128)}, u32[]{:S(2)}) copy-start(s32[1,52]{1,0:T(1,128)} %param.11) | copy-start | bytes 628
  129.3 13.7 %copy-start.1 = (bf16[16,16]{1,0:T(8,128)(2,1)S(1)}, bf16[16,16]{1,0:T(8,128)(2,1)}, u32[]{:S(2)}) copy-start(bf16[16,16]{1,0:T(8,128)(2,1)} %param.13) | copy-start | bytes 1540
  141.0 60.1 %collective-permute-start.7 = (bf16[16,52,512]{2,0,1:T(8,128)(2,1)}, bf16[16,52,512]{2,0,1:T(8,128)(2,1)}, u32[]{:S(2)}, u32[]{:S(2)}) collective-permute-start(bf16[16,52,512]{2,0,1:T(8,128)(2,1)} %collective-permute-done.6), channel_id=1, source_target_pairs={{508,0},{0,4},{4,8},{8,12},{12,16},{16,20},{20,24},{24,28},{28,32}... | collective-permute-start | bytes 2555912 | tf_op jit(solution)/shard_map/ppermute | solution.py:17
  188.3 18.5 %collective-permute-start.10 = (f32[16,16]{1,0:T(8,128)S(1)}, f32[16,16]{1,0:T(8,128)S(1)}, u32[]{:S(2)}, u32[]{:S(2)}) collective-permute-start(f32[16,16]{1,0:T(8,128)S(1)} %bitcast.143), channel_id=1, source_target_pairs={{12,0},{16,4},{20,8},{24,12},{28,16},{32,20},{36,24},{40,28},{44,3... | collective-permute-start | bytes 3080 | tf_op jit(solution)/shard_map/ppermute | solution.py:17
  192.6 14.9 %collective-permute-start.9 = (f32[16,16]{1,0:T(8,128)S(1)}, f32[16,16]{1,0:T(8,128)S(1)}, u32[]{:S(2)}, u32[]{:S(2)}) collective-permute-start(f32[16,16]{1,0:T(8,128)S(1)} %bitcast.144), channel_id=1, source_target_pairs={{8,0},{12,4},{16,8},{20,12},{24,16},{28,20},{32,24},{36,28},{40,32... | collective-permute-start | bytes 3080 | tf_op jit(solution)/shard_map/ppermute | solution.py:17
  196.8 10.6 %collective-permute-start.8 = (f32[16,16]{1,0:T(8,128)S(1)}, f32[16,16]{1,0:T(8,128)S(1)}, u32[]{:S(2)}, u32[]{:S(2)}) collective-permute-start(f32[16,16]{1,0:T(8,128)S(1)} %bitcast.145), channel_id=1, source_target_pairs={{4,0},{8,4},{12,8},{16,12},{20,16},{24,20},{28,24},{32,28},{36,32}... | collective-permute-start | bytes 3080 | tf_op jit(solution)/shard_map/ppermute | solution.py:17
  202.9 14.6 %collective-permute-start.11 = (f32[16,16]{1,0:T(8,128)S(1)}, f32[16,16]{1,0:T(8,128)S(1)}, u32[]{:S(2)}, u32[]{:S(2)}) collective-permute-start(f32[16,16]{1,0:T(8,128)S(1)} %bitcast.146), channel_id=1, source_target_pairs={{16,0},{20,4},{24,8},{28,12},{32,16},{36,20},{40,24},{44,28},{48,3... | collective-permute-start | bytes 3080 | tf_op jit(solution)/shard_map/ppermute | solution.py:17
where the time goes:
time: 229 us; the launch traced here: 228 us
  local copies, waits for them, and re-layouts  90 us (39%)
  starting transfers between devices  75.1 us (33%)
  waiting for transfers between devices  29 us (13%)
  matrix products  19.2 us (8%)
  blocking collectives  8.13 us (4%)
  between operations  3.47 us (2%)
  other arithmetic  2.69 us (1%)
    ppermute x12, starting transfers between devices, from_behind(): return lax.ppermute(block, axis, route)  61.9 us
    all_to_all x1, waiting for transfers between devices, body(): lax.all_to_all(smooth_depth(lax.all_to_all(sensitivity, 'cell', split_axi...  16.7 us
    unnamed x12, local copies, waits for them, and re-layouts  16.3 us
    broadcast_in_dim x4, local copies, waits for them, and re-layouts, smooth_plane(): lax.map(smooth_group, grouped).reshape(row_count, tile_count, slab_width)  14.3 us
    reshape x1, local copies, waits for them, and re-layouts, smooth_depth(): smoothed.astype(jnp.bfloat16).reshape(row_count, tile_count, slab_width)  12.5 us
    ppermute x12, waiting for transfers between devices, from_behind(): return lax.ppermute(block, axis, route)  12.3 us
    reshape x8, local copies, waits for them, and re-layouts, smooth_group(): row_group.reshape(group_rows, cells_across, blocks_along, slab_width // T...  11.4 us
    all_to_all x2, local copies, waits for them, and re-layouts, body(): lax.all_to_all(smooth_depth(lax.all_to_all(sensitivity, 'cell', split_axi...  9.47 us
  transfers between devices with their start and end apart: 14, of which 5 were waited for; matrix products, arithmetic and copies ran while one was open for 48% of the time, Pallas kernels for 0%

commit v1 on v0

v1 whole, which is shorter than its diff:
```python
import jax
import jax.numpy as jnp
from jax import lax
from jax.experimental import pallas as pl
from jax.experimental.pallas import tpu as pltpu
from jax.sharding import PartitionSpec as P

TILE = 16
FOOT = 52
TILES = 64
BAND = 9
ROWS = 16
WIDTH = 512
CELLS = 4
STAS = 128
PART = FOOT // CELLS
CHUNKS = ((0, 7), (7, 6))
SHARE = BAND * ROWS // CELLS
MESH = pl.DeviceIdType.MESH
OWN, BEHIND, BESIDE, ASIDE, FAR = range(5)
SLOTS = 5
F32, BF16 = jnp.float32, jnp.bfloat16


def iota(shape, dim):
    return lax.broadcasted_iota(jnp.int32, shape, dim)


def dot(a, b):
    return jnp.dot(a, b, preferred_element_type=F32)


def kron_rows(small_ref, wide_ref, big_ref):
    n = small_ref.shape[0]
    repeat = (iota((n, n * TILE), 0) == iota((n, n * TILE), 1) // TILE).astype(BF16)
    wide_ref[...] = dot(small_ref[...], repeat)
    same = iota((TILE, n * TILE), 0) == iota((TILE, n * TILE), 1) % TILE

    def row(a, carry):
        line = jnp.broadcast_to(wide_ref[pl.ds(a, 1), :], (TILE, n * TILE))
        big_ref[pl.ds(pl.multiple_of(a * TILE, TILE), TILE), :] = jnp.where(same, line, 0.0).astype(BF16)
        return carry

    lax.fori_loop(0, n, row, 0)


def kernel(
    x_hbm, inv_own, foot_own, inv_vmem, link, sx, sy, sz, out,
    held, tables, inv_smem, first, second, smoothed, wz, kx, ky, wide_z, wide_x,
    dense, across, field, square, turned, turned_in, shares, shares_in,
    z1_send, z1_recv, z2_send, z2_recv, h_send, h_recv, t_send, t_recv,
    b_send, b_recv, c_send, c_recv, local,
):
    s = lax.axis_index("sta")
    c = lax.axis_index("cell")
    odd = lax.rem(s, 2)

    def at(distance):
        return lax.rem(s + distance + STAS, STAS)

    def remote(src, dst, send, recv, sta, cell):
        return pltpu.make_async_remote_copy(
            src_ref=src, dst_ref=dst, send_sem=send, recv_sem=recv,
            device_id=(sta, cell), device_id_type=MESH,
        )

    sibling = s + 1 - 2 * odd
    aside_to = at(-3 + 2 * odd)

    barrier = pltpu.get_barrier_semaphore()
    for distance in (-4, -3, -2, -1, 1, 2, 3, 4):
        pl.semaphore_signal(barrier, inc=1, device_id=(at(distance), c), device_id_type=MESH)
    for j in (1, 2, 3):
        pl.semaphore_signal(barrier, inc=1, device_id=(s, lax.rem(c + j, CELLS)), device_id_type=MESH)
    pl.semaphore_wait(barrier, 11)

    def send_first(j, k):
        f0, fn = CHUNKS[k]
        to = lax.rem(c + j, CELLS)
        return remote(
            x_hbm.at[pl.ds(to * PART + f0, fn)], first.at[c, pl.ds(f0, fn)],
            z1_send.at[j - 1, k], z1_recv.at[j - 1, k], s, to,
        )

    def recv_first(j, k):
        f0, fn = CHUNKS[k]
        came = lax.rem(c + CELLS - j, CELLS)
        return remote(
            x_hbm.at[pl.ds(f0, fn)], first.at[came, pl.ds(f0, fn)],
            z1_send.at[j - 1, k], z1_recv.at[j - 1, k], s, came,
        )

    for k in range(len(CHUNKS)):
        for j in (2, 1, 3):
            send_first(j, k).start()

    def halo(slot, src, sta):
        return remote(src, held[slot].at[pl.ds(0, FOOT)], h_send.at[slot], h_recv.at[slot], sta, c)

    def table(slot, src, sta):
        return remote(src, tables[slot], t_send.at[slot], t_recv.at[slot], sta, c)

    sent_behind = halo(BEHIND, x_hbm, at(2))
    sent_behind.start()
    sent_table_behind = table(BEHIND, inv_vmem, at(2))
    sent_table_behind.start()
    sent_aside = halo(ASIDE, x_hbm, aside_to)
    sent_aside.start()
    sent_table_aside = table(ASIDE, inv_vmem, aside_to)
    sent_table_aside.start()

    own_first = pltpu.make_async_copy(x_hbm.at[pl.ds(c * PART, PART)], first.at[c], local.at[0])
    own_first.start()
    own_held = pltpu.make_async_copy(x_hbm, held[OWN].at[pl.ds(0, FOOT)], local.at[1])
    own_held.start()
    for slot in range(SLOTS):
        held[slot][FOOT] = jnp.zeros((ROWS, WIDTH), BF16)

    kron_rows(sx, wide_x, kx)
    wide = iota((TILES, WIDTH), 1)
    spread = (iota((TILES, WIDTH), 0) == (wide // 128) * TILE + wide % TILE).astype(BF16)
    rows_y = dot(sy[...], spread)
    level = (iota((TILE, WIDTH), 1) // TILE) % 8
    for b in range(4):
        for z in range(8):
            ky[(b * 8 + z) * TILE : (b * 8 + z + 1) * TILE, :] = jnp.where(
                level == z, rows_y[b * TILE : (b + 1) * TILE, :], 0.0
            ).astype(BF16)
    kron_rows(sz, wide_z, wz)

    def smooth_plane(slot, index):
        def along_x(b, carry):
            for x in range(16):
                dense[x * ROWS : (x + 1) * ROWS, :] = held[slot][index(b * 16 + x)]
            mixed = dot(kx[...], dense[...]).astype(BF16)
            for g in range(4):
                across[g, :, pl.ds(pl.multiple_of(b * 128, 128), 128)] = mixed[:, g * 128 : (g + 1) * 128]
            return carry

        lax.fori_loop(0, 4, along_x, 0)

        def along_y(g, carry):
            mixed = dot(across[g], ky[...]).astype(BF16)
            for e in range(4):
                field[
                    e * 16 : (e + 1) * 16, slot * ROWS : (slot + 1) * ROWS, pl.ds(pl.multiple_of(g * 128, 128), 128)
                ] = mixed[:, e * 128 : (e + 1) * 128].reshape(16, ROWS, 128)
            return carry

        lax.fori_loop(0, 4, along_y, 0)

    def take_table(slot):
        copy = pltpu.make_async_copy(tables[slot], inv_smem[slot], local.at[2 + slot])
        copy.start()
        copy.wait()

    own_held.wait()
    smooth_plane(OWN, lambda i: inv_own[0, i])

    def send_second(j, k):
        f0, fn = CHUNKS[k]
        to = lax.rem(c + j, CELLS)
        return remote(
            second.at[to, pl.ds(f0, fn)], smoothed.at[pl.ds(c * PART + f0, fn)],
            z2_send.at[j - 1, k], z2_recv.at[j - 1, k], s, to,
        )

    def recv_second(j, k):
        f0, fn = CHUNKS[k]
        came = lax.rem(c + CELLS - j, CELLS)
        return remote(
            second.at[came, pl.ds(f0, fn)], smoothed.at[pl.ds(came * PART + f0, fn)],
            z2_send.at[j - 1, k], z2_recv.at[j - 1, k], s, came,
        )

    def own_second(k):
        f0, fn = CHUNKS[k]
        return pltpu.make_async_copy(
            second.at[c, pl.ds(f0, fn)], smoothed.at[pl.ds(c * PART + f0, fn)], local.at[7 + k]
        )

    def smooth_depth(k):
        f0, fn = CHUNKS[k]
        for j in (1, 2, 3):
            recv_first(j, k).wait_recv()
        if k == 0:
            own_first.wait()
        rows = jnp.concatenate(
            [first[d, f0 : f0 + fn].reshape(fn * ROWS, WIDTH) for d in range(CELLS)], axis=1
        )
        for j in (2, 1, 3, 0):
            to = lax.rem(c + j, CELLS)
            done = dot(rows, wz[:, pl.ds(pl.multiple_of(to * WIDTH, WIDTH), WIDTH)])
            second[to, f0 : f0 + fn] = done.astype(BF16).reshape(fn, ROWS, WIDTH)
            if j:
                send_second(j, k).start()
            else:
                own_second(k).start()

    smooth_depth(0)

    halo(ASIDE, x_hbm, aside_to).wait_recv()
    table(ASIDE, inv_vmem, aside_to).wait_recv()
    take_table(ASIDE)
    smooth_plane(ASIDE, lambda i: inv_smem[ASIDE][0, i])

    halo(BEHIND, x_hbm, at(2)).wait_recv()
    table(BEHIND, inv_vmem, at(2)).wait_recv()
    came = held[BEHIND].at[pl.ds(0, FOOT)]
    sent_far = halo(FAR, came, at(2))
    sent_far.start()
    sent_table_far = table(FAR, tables[BEHIND], at(2))
    sent_table_far.start()
    sent_beside = halo(BESIDE, came, sibling)
    sent_beside.start()
    sent_table_beside = table(BESIDE, tables[BEHIND], sibling)
    sent_table_beside.start()
    take_table(BEHIND)
    smooth_plane(BEHIND, lambda i: inv_smem[BEHIND][0, i])

    smooth_depth(1)

    sent_beside.wait_recv()
    sent_table_beside.wait_recv()
    take_table(BESIDE)
    smooth_plane(BESIDE, lambda i: inv_smem[BESIDE][0, i])

    sent_far.wait_recv()
    sent_table_far.wait_recv()
    take_table(FAR)
    smooth_plane(FAR, lambda i: inv_smem[FAR][0, i])

    total = jnp.zeros((ROWS, SLOTS * ROWS), F32)
    for k, (f0, fn) in enumerate(CHUNKS):
        own_second(k).wait()
        for j in (1, 2, 3):
            recv_second(j, k).wait_recv()

        def product(e, total, f0=f0, fn=fn):
            for f in range(f0, f0 + fn):
                place = e * PART + f
                total = total + lax.dot_general(
                    smoothed[place], field[foot_own[0, place]],
                    (((1,), (1,)), ((), ())), preferred_element_type=F32,
                )
            return total

        total = lax.fori_loop(0, CELLS, product, total)

    square[...] = jnp.zeros((128, 128), F32)
    square[0:ROWS, 0 : SLOTS * ROWS] = total
    flipped = square[...].T
    back = {}
    for i, slot in enumerate((BEHIND, BESIDE, FAR, ASIDE)):
        turned[i] = flipped[slot * ROWS : (slot + 1) * ROWS, :]
    partners = (at(-2), at(-1 - 2 * odd), at(-4), at(1 + 2 * odd))
    for i in range(4):
        back[i] = remote(turned.at[i], turned_in.at[i], b_send.at[i], b_recv.at[i], partners[i], c)
        back[i].start()
    for i in range(4):
        back[i].wait_recv()

    def mine(slot):
        return total[:, slot * ROWS : (slot + 1) * ROWS]

    def theirs(i):
        return turned_in[i][:, :ROWS]

    is_odd = odd == 1
    beside, aside = mine(BESIDE), mine(ASIDE)
    parts = [
        mine(FAR),
        jnp.where(is_odd, beside, theirs(3)),
        mine(BEHIND),
        jnp.where(is_odd, theirs(3), beside),
        mine(OWN),
        jnp.where(is_odd, theirs(1), aside),
        theirs(0),
        jnp.where(is_odd, aside, theirs(1)),
        theirs(2),
    ]
    whole = jnp.concatenate(parts, axis=1) * link[0:1, 0 : BAND * ROWS]
    for e in range(CELLS):
        shares[e, :, 0:SHARE] = whole[:, e * SHARE : (e + 1) * SHARE]
    given = []
    for j in (1, 2, 3):
        to = lax.rem(c + j, CELLS)
        copy = remote(shares.at[to], shares_in.at[j - 1], c_send.at[j - 1], c_recv.at[j - 1], s, to)
        copy.start()
        given.append(copy)
    for copy in given:
        copy.wait_recv()
    summed = shares[c] + shares_in[0] + shares_in[1] + shares_in[2]
    out[...] = summed[:, 0:SHARE]

    for k in range(len(CHUNKS)):
        for j in (1, 2, 3):
            send_first(j, k).wait_send()
            send_second(j, k).wait_send()
    for copy in (
        sent_behind, sent_table_behind, sent_aside, sent_table_aside,
        sent_far, sent_table_far, sent_beside, sent_table_beside,
        *back.values(), *given,
    ):
        copy.wait_send()


def body(sensitivity, footprint, linked, smooth_x, smooth_y, smooth_z):
    values = jnp.transpose(sensitivity, (1, 0, 2))
    tiles = jnp.arange(TILES, dtype=jnp.int32)
    tile_of = (tiles % 16) * 4 + tiles // 16
    match = footprint[0][None, :] == tile_of[:, None]
    order = jnp.arange(FOOT, dtype=jnp.int32)[None, :]
    inverse = FOOT + jnp.sum(jnp.where(match, order - FOOT, 0), axis=1)
    inverse = jnp.broadcast_to(jnp.pad(inverse, (0, 128 - TILES))[None, :], (8, 128))
    foot = (footprint % 4) * 16 + footprint // 4
    link = jnp.repeat(linked.astype(F32), ROWS, axis=1)
    n_k = len(CHUNKS)
    vmem = pl.BlockSpec(memory_space=pltpu.VMEM)
    smem = pl.BlockSpec(memory_space=pltpu.SMEM)
    dma = pltpu.SemaphoreType.DMA
    return pl.pallas_call(
        kernel,
        out_shape=jax.ShapeDtypeStruct((ROWS, SHARE), F32),
        in_specs=[pl.BlockSpec(memory_space=pl.ANY), smem, smem, vmem, vmem, vmem, vmem, vmem],
        out_specs=vmem,
        scratch_shapes=[
            [pltpu.VMEM((FOOT + 1, ROWS, WIDTH), BF16)] * SLOTS,
            [pltpu.VMEM((8, 128), jnp.int32)] * SLOTS,
            [pltpu.SMEM((8, 128), jnp.int32)] * SLOTS,
            pltpu.VMEM((CELLS, PART, ROWS, WIDTH), BF16),
            pltpu.VMEM((CELLS, PART, ROWS, WIDTH), BF16),
            pltpu.VMEM((FOOT, ROWS, WIDTH), BF16),
            pltpu.VMEM((2048, 2048), BF16),
            pltpu.VMEM((256, 256), BF16),
            pltpu.VMEM((512, 512), BF16),
            pltpu.VMEM((128, 2048), F32),
            pltpu.VMEM((16, 256), F32),
            pltpu.VMEM((256, WIDTH), BF16),
            pltpu.VMEM((4, 256, WIDTH), BF16),
            pltpu.VMEM((TILES, SLOTS * ROWS, WIDTH), BF16),
            pltpu.VMEM((128, 128), F32),
            pltpu.VMEM((4, ROWS, 128), F32),
            pltpu.VMEM((4, ROWS, 128), F32),
            pltpu.VMEM((CELLS, ROWS, 128), F32),
            pltpu.VMEM((CELLS - 1, ROWS, 128), F32),
            dma((3, n_k)), dma((3, n_k)), dma((3, n_k)), dma((3, n_k)),
            dma((SLOTS,)), dma((SLOTS,)), dma((SLOTS,)), dma((SLOTS,)),
            dma((4,)), dma((4,)), dma((3,)), dma((3,)), dma((10,)),
        ],
        compiler_params=pltpu.CompilerParams(
            collective_id=0, has_side_effects=True, vmem_limit_bytes=56 * 2**20
        ),
        name="band",
    )(values, inverse, foot, inverse, link, smooth_x, smooth_y, smooth_z)


def solution(mesh):
    return jax.shard_map(
        body,
        mesh=mesh,
        in_specs=(P("sta", None, "cell"), P("sta", None), P("sta", None), P(), P(), P()),
        out_specs=P("sta", "cell"),
        check_vma=False,
    )
```

time: 229 us -> 141 us (0.62)
  the two profiles are of different devices: /device:TPU:62 before, /device:TPU:260 now
where the time goes in v1:
time: 141 us
  Pallas kernels  136 us (96%)
  local copies, waits for them, and re-layouts  3.93 us (3%)
    pallas_call x1, Pallas kernels, body(): pl.pallas_call(kernel, out_shape=jax.ShapeDtypeStruct((ROWS, SHARE), F32)...  136 us

profile of v1, /device:TPU:260, one launch (start us, length us, event | category | flops | bytes accessed | tf_op | source)
XLA Modules:
  0.0 140.8 jit_solution(11175658329526469269)
XLA Ops:
  0.0 0.0 copy-start.1
  0.0 0.7 copy-done.1
  0.7 0.0 copy-start
  0.7 0.7 copy-done
  1.3 0.5 fusion.3.foot_own
  1.9 0.1 select_reduce_fusion
  2.0 0.6 broadcast_in_dim.27.inv_own.inv_vmem
  2.6 0.1 broadcast_in_dim.28
  2.7 0.7 broadcast_in_dim.29.link
  3.3 136.1 %band.1 = f32[16,36]{1,0:T(8,128)} custom-call(bf16[52,16,512]{2,1,0:T(8,128)(2,1)} %bitcast.4, s32[8,128]{1,0:T(8,128)} %broadcast_in_dim.27.inv_own.inv_vmem, s32[1,52]{1,0:T(1,128)} %fusion.3.foot_own, s32[8,128]{1,0:T(8,128)} %broadcast_in_dim.27.inv_own.inv_vmem, f32[1,144]{1,0:T(1,128)} %broadcast_in_dim.29.link, bf16[16,16]{1,0:T(8,128)(2,1)} %sx.1, ...), custom_call_target="tpu_custom_call" | custom-call | tf_op jit(solution)/shard_map/band/pallas_call | solution.py:322
  139.5 1.3 copy.8
  (5 shorter events, 0.0 us)
Async XLA Ops:
  0.0 0.7 copy-start.1
  0.7 0.7 copy-start

commit v2 on v1

--- a/solution.py
+++ b/solution.py
@@ -20,6 +20,26 @@
 OWN, BEHIND, BESIDE, ASIDE, FAR = range(5)
 SLOTS = 5
 F32, BF16 = jnp.float32, jnp.bfloat16
+PIECES = {BEHIND: 4, BESIDE: 1, ASIDE: 2, FAR: 4}
+HALF_STAS = 64
+
+
+def crossings():
+    flows = []
+    for k in range(2):
+        for slot, source, column in ((BEHIND, 62 + k, k), (FAR, 60 + k, 2 + k)):
+            flows.append((slot, 0, source, None, k))
+            for p, row in enumerate((1, 7, 6), 1):
+                flows.append((slot, p, source, 8 * row + column, k))
+    for source, relay, target in ((0, 53, 61), (2, 52, 63)):
+        flows.append((ASIDE, 0, source, None, target))
+        flows.append((ASIDE, 1, source, relay, target))
+    return flows
+
+
+FLOWS = crossings()
+SOURCES = sorted({flow[2] for flow in FLOWS})
+RELAYED = [flow for flow in FLOWS if flow[3] is not None]
 
 
 def iota(shape, dim):
@@ -49,7 +69,7 @@
     held, tables, inv_smem, first, second, smoothed, wz, kx, ky, wide_z, wide_x,
     dense, across, field, square, turned, turned_in, shares, shares_in,
     z1_send, z1_recv, z2_send, z2_recv, h_send, h_recv, t_send, t_recv,
-    b_send, b_recv, c_send, c_recv, local,
+    b_send, b_recv, c_send, c_recv, local, relay, cross_send, relay_send, relay_recv,
 ):
     s = lax.axis_index("sta")
     c = lax.axis_index("cell")
@@ -66,13 +86,28 @@
 
     sibling = s + 1 - 2 * odd
     aside_to = at(-3 + 2 * odd)
+    place = lax.rem(s, HALF_STAS)
+    here = s - place
+    beyond = HALF_STAS - here
 
     barrier = pltpu.get_barrier_semaphore()
     for distance in (-4, -3, -2, -1, 1, 2, 3, 4):
         pl.semaphore_signal(barrier, inc=1, device_id=(at(distance), c), device_id_type=MESH)
     for j in (1, 2, 3):
         pl.semaphore_signal(barrier, inc=1, device_id=(s, lax.rem(c + j, CELLS)), device_id_type=MESH)
-    pl.semaphore_wait(barrier, 11)
+    for slot, p, source, relay_at, target in RELAYED:
+        @pl.when(place == relay_at)
+        def _(source=source):
+            pl.semaphore_signal(barrier, inc=1, device_id=(beyond + source, c), device_id_type=MESH)
+
+        @pl.when(place == target)
+        def _(relay_at=relay_at):
+            pl.semaphore_signal(barrier, inc=1, device_id=(here + relay_at, c), device_id_type=MESH)
+
+    greeted = jnp.int32(11)
+    for slot, p, source, relay_at, target in RELAYED:
+        greeted += jnp.where(jnp.logical_or(place == relay_at, place == source), 1, 0)
+    pl.semaphore_wait(barrier, greeted)
 
     def send_first(j, k):
         f0, fn = CHUNKS[k]
@@ -94,20 +129,60 @@
         for j in (2, 1, 3):
             send_first(j, k).start()
 
-    def halo(slot, src, sta):
-        return remote(src, held[slot].at[pl.ds(0, FOOT)], h_send.at[slot], h_recv.at[slot], sta, c)
-
-    def table(slot, src, sta):
-        return remote(src, tables[slot], t_send.at[slot], t_recv.at[slot], sta, c)
-
-    sent_behind = halo(BEHIND, x_hbm, at(2))
-    sent_behind.start()
-    sent_table_behind = table(BEHIND, inv_vmem, at(2))
-    sent_table_behind.start()
-    sent_aside = halo(ASIDE, x_hbm, aside_to)
-    sent_aside.start()
-    sent_table_aside = table(ASIDE, inv_vmem, aside_to)
-    sent_table_aside.start()
+    def cut(slot, p):
+        size = FOOT // PIECES[slot]
+        return pl.ds(p * size, size)
+
+    def halo(slot, p, src, send, sta):
+        return remote(src.at[cut(slot, p)], held[slot].at[cut(slot, p)], send, h_recv.at[slot, p], sta, c)
+
+    def halos(slot, src, sta):
+        return [halo(slot, p, src, h_send.at[slot, p], sta) for p in range(PIECES[slot])]
+
+    def begin(copies):
+        for copy in copies:
+            copy.start()
+
+    def to_relay(slot, p, send, sta):
+        size = FOOT // PIECES[slot]
+        return remote(x_hbm.at[cut(slot, p)], relay.at[pl.ds(0, size)], send, relay_recv.at[0], sta, c)
+
+    def from_relay(slot, p, sta):
+        size = FOOT // PIECES[slot]
+        return remote(
+            relay.at[pl.ds(0, size)], held[slot].at[cut(slot, p)], relay_send.at[0], h_recv.at[slot, p], sta, c
+        )
+
+    def table(slot, sta):
+        return remote(inv_vmem, tables[slot], t_send.at[slot], t_recv.at[slot], sta, c)
+
+    sent_tables = [
+        table(BEHIND, at(2)), table(BESIDE, at(3 - 2 * odd)), table(ASIDE, aside_to), table(FAR, at(4))
+    ]
+    begin(sent_tables)
+    sent_behind = halos(BEHIND, x_hbm, at(2))
+    sent_aside = halos(ASIDE, x_hbm, aside_to)
+    inner = place < 62
+    straight = jnp.logical_and(place != 0, place != 2)
+
+    @pl.when(inner)
+    def _():
+        begin(sent_behind)
+
+    @pl.when(straight)
+    def _():
+        begin(sent_aside)
+
+    for source_at in SOURCES:
+        @pl.when(place == source_at)
+        def _(source_at=source_at):
+            for slot, p, source, relay_at, target in FLOWS:
+                if source == source_at:
+                    send = cross_send.at[p] if slot == FAR else h_send.at[slot, p]
+                    if relay_at is None:
+                        halo(slot, p, x_hbm, send, beyond + target).start()
+                    else:
+                        to_relay(slot, p, send, beyond + relay_at).start()
 
     own_first = pltpu.make_async_copy(x_hbm.at[pl.ds(c * PART, PART)], first.at[c], local.at[0])
     own_first.start()
@@ -199,34 +274,42 @@
 
     smooth_depth(0)
 
-    halo(ASIDE, x_hbm, aside_to).wait_recv()
-    table(ASIDE, inv_vmem, aside_to).wait_recv()
+    for p in range(PIECES[ASIDE]):
+        sent_aside[p].wait_recv()
+    sent_tables[2].wait_recv()
     take_table(ASIDE)
     smooth_plane(ASIDE, lambda i: inv_smem[ASIDE][0, i])
 
-    halo(BEHIND, x_hbm, at(2)).wait_recv()
-    table(BEHIND, inv_vmem, at(2)).wait_recv()
-    came = held[BEHIND].at[pl.ds(0, FOOT)]
-    sent_far = halo(FAR, came, at(2))
-    sent_far.start()
-    sent_table_far = table(FAR, tables[BEHIND], at(2))
-    sent_table_far.start()
-    sent_beside = halo(BESIDE, came, sibling)
-    sent_beside.start()
-    sent_table_beside = table(BESIDE, tables[BEHIND], sibling)
-    sent_table_beside.start()
+    for slot, p, source, relay_at, target in RELAYED:
+        @pl.when(place == relay_at)
+        def _(slot=slot, p=p, source=source, target=target):
+            to_relay(slot, p, h_send.at[BEHIND, 0], beyond + source).wait_recv()
+            from_relay(slot, p, here + target).start()
+
+    sent_far = halos(FAR, held[BEHIND], at(2))
+    for p in range(PIECES[BEHIND]):
+        sent_behind[p].wait_recv()
+
+        @pl.when(inner)
+        def _(p=p):
+            sent_far[p].start()
+
+    sent_beside = halos(BESIDE, held[BEHIND], sibling)
+    begin(sent_beside)
+    sent_tables[0].wait_recv()
     take_table(BEHIND)
     smooth_plane(BEHIND, lambda i: inv_smem[BEHIND][0, i])
 
     smooth_depth(1)
 
-    sent_beside.wait_recv()
-    sent_table_beside.wait_recv()
+    sent_beside[0].wait_recv()
+    sent_tables[1].wait_recv()
     take_table(BESIDE)
     smooth_plane(BESIDE, lambda i: inv_smem[BESIDE][0, i])
 
-    sent_far.wait_recv()
-    sent_table_far.wait_recv()
+    for p in range(PIECES[FAR]):
+        sent_far[p].wait_recv()
+    sent_tables[3].wait_recv()
     take_table(FAR)
     smooth_plane(FAR, lambda i: inv_smem[FAR][0, i])
 
@@ -297,12 +380,23 @@
         for j in (1, 2, 3):
             send_first(j, k).wait_send()
             send_second(j, k).wait_send()
-    for copy in (
-        sent_behind, sent_table_behind, sent_aside, sent_table_aside,
-        sent_far, sent_table_far, sent_beside, sent_table_beside,
-        *back.values(), *given,
-    ):
+    for copy in (*sent_tables, *sent_behind, *sent_aside, *sent_beside, *back.values(), *given):
         copy.wait_send()
+
+    @pl.when(inner)
+    def _():
+        for copy in sent_far:
+            copy.wait_send()
+
+    @pl.when(jnp.logical_or(place == 60, place == 61))
+    def _():
+        for p in range(PIECES[FAR]):
+            halo(FAR, p, x_hbm, cross_send.at[p], beyond).wait_send()
+
+    for slot, p, source, relay_at, target in RELAYED:
+        @pl.when(place == relay_at)
+        def _(slot=slot, p=p, target=target):
+            from_relay(slot, p, here + target).wait_send()
 
 
 def body(sensitivity, footprint, linked, smooth_x, smooth_y, smooth_z):
@@ -345,8 +439,9 @@
             pltpu.VMEM((CELLS, ROWS, 128), F32),
             pltpu.VMEM((CELLS - 1, ROWS, 128), F32),
             dma((3, n_k)), dma((3, n_k)), dma((3, n_k)), dma((3, n_k)),
-            dma((SLOTS,)), dma((SLOTS,)), dma((SLOTS,)), dma((SLOTS,)),
+            dma((SLOTS, 4)), dma((SLOTS, 4)), dma((SLOTS,)), dma((SLOTS,)),
             dma((4,)), dma((4,)), dma((3,)), dma((3,)), dma((10,)),
+            pltpu.VMEM((FOOT // 2, ROWS, WIDTH), BF16), dma((4,)), dma((1,)), dma((1,)),
         ],
         compiler_params=pltpu.CompilerParams(
             collective_id=0, has_side_effects=True, vmem_limit_bytes=56 * 2**20

time: 141 us -> 93.6 us (0.66)
  the two profiles are of different devices: /device:TPU:260 before, /device:TPU:2 now
where the time goes in v2:
time: 93.6 us; the launch traced here: 93.4 us
  Pallas kernels  88.8 us (95%)
  local copies, waits for them, and re-layouts  3.93 us (4%)
    pallas_call x1, Pallas kernels, body(): pl.pallas_call(kernel, out_shape=jax.ShapeDtypeStruct((ROWS, SHARE), F32)...  88.8 us
    unnamed x5, local copies, waits for them, and re-layouts  2.6 us

profile of v2, /device:TPU:2, one launch (start us, length us, event | category | flops | bytes accessed | tf_op | source)
XLA Modules:
  0.0 93.4 jit_solution(15428695516471466907)
XLA Ops:
  0.0 0.0 copy-start.1
  0.0 0.7 copy-done.1
  0.7 0.0 copy-start
  0.7 0.7 copy-done
  1.3 0.5 fusion.3.foot_own
  1.9 0.1 select_reduce_fusion
  2.0 0.6 broadcast_in_dim.27.inv_own.inv_vmem
  2.6 0.1 broadcast_in_dim.28
  2.7 0.7 broadcast_in_dim.29.link
  3.3 88.8 %band.1 = f32[16,36]{1,0:T(8,128)} custom-call(bf16[52,16,512]{2,1,0:T(8,128)(2,1)} %bitcast.4, s32[8,128]{1,0:T(8,128)} %broadcast_in_dim.27.inv_own.inv_vmem, s32[1,52]{1,0:T(1,128)} %fusion.3.foot_own, s32[8,128]{1,0:T(8,128)} %broadcast_in_dim.27.inv_own.inv_vmem, f32[1,144]{1,0:T(1,128)} %broadcast_in_dim.29.link, bf16[16,16]{1,0:T(8,128)(2,1)} %sx.1, ...), custom_call_target="tpu_custom_call" | custom-call | tf_op jit(solution)/shard_map/band/pallas_call | solution.py:416
  92.1 1.3 %copy.8 = f32[16,36]{1,0:T(8,128)} copy(f32[16,36]{1,0:T(8,128)} %band.1) | data formatting | bytes 4608
  (5 shorter events, 0.0 us)
Async XLA Ops:
  0.0 0.7 copy-start.1
  0.7 0.7 copy-start

commit v3 on v2

--- a/solution.py
+++ b/solution.py
@@ -26,11 +26,10 @@
 
 def crossings():
     flows = []
-    for k in range(2):
-        for slot, source, column in ((BEHIND, 62 + k, k), (FAR, 60 + k, 2 + k)):
-            flows.append((slot, 0, source, None, k))
-            for p, row in enumerate((1, 7, 6), 1):
-                flows.append((slot, p, source, 8 * row + column, k))
+    for slot, source, column, target in ((BEHIND, 62, 0, 0), (BEHIND, 63, 1, 1), (FAR, 61, 3, 1)):
+        flows.append((slot, 0, source, None, target))
+        for p, row in enumerate((1, 7, 6), 1):
+            flows.append((slot, p, source, 8 * row + column, target))
     for source, relay, target in ((0, 53, 61), (2, 52, 63)):
         flows.append((ASIDE, 0, source, None, target))
         flows.append((ASIDE, 1, source, relay, target))
@@ -70,6 +69,7 @@
     dense, across, field, square, turned, turned_in, shares, shares_in,
     z1_send, z1_recv, z2_send, z2_recv, h_send, h_recv, t_send, t_recv,
     b_send, b_recv, c_send, c_recv, local, relay, cross_send, relay_send, relay_recv,
+    hop, hop_send, hop_recv, over_send,
 ):
     s = lax.axis_index("sta")
     c = lax.axis_index("cell")
@@ -157,21 +157,35 @@
         return remote(inv_vmem, tables[slot], t_send.at[slot], t_recv.at[slot], sta, c)
 
     sent_tables = [
-        table(BEHIND, at(2)), table(BESIDE, at(3 - 2 * odd)), table(ASIDE, aside_to), table(FAR, at(4))
+        table(BEHIND, at(2)), table(BESIDE, at(3 - 2 * odd)), table(ASIDE, aside_to), table(FAR, at(8 * odd - 4))
     ]
     begin(sent_tables)
     sent_behind = halos(BEHIND, x_hbm, at(2))
     sent_aside = halos(ASIDE, x_hbm, aside_to)
+    sent_far = halos(FAR, held[BEHIND], at(2))
+    over_far = [halo(FAR, p, held[ASIDE], over_send.at[p], sibling) for p in range(PIECES[FAR])]
+    sent_beside = halos(BESIDE, held[BEHIND], sibling)
     inner = place < 62
-    straight = jnp.logical_and(place != 0, place != 2)
+    is_odd = odd == 1
+    hopping = jnp.logical_and(odd == 0, place >= 4)
+    hops = jnp.logical_and(odd == 0, jnp.logical_and(place >= 2, place <= 60))
+    sent_hop = [
+        remote(x_hbm.at[cut(ASIDE, p)], hop.at[cut(ASIDE, p)], h_send.at[ASIDE, p], hop_recv.at[p], at(-2), c)
+        for p in range(PIECES[ASIDE])
+    ]
+    past_hop = [halo(ASIDE, p, hop, hop_send.at[p], at(-1)) for p in range(PIECES[ASIDE])]
 
     @pl.when(inner)
     def _():
         begin(sent_behind)
 
-    @pl.when(straight)
+    @pl.when(is_odd)
     def _():
         begin(sent_aside)
+
+    @pl.when(hopping)
+    def _():
+        begin(sent_hop)
 
     for source_at in SOURCES:
         @pl.when(place == source_at)
@@ -272,13 +286,13 @@
             else:
                 own_second(k).start()
 
+    @pl.when(hops)
+    def _():
+        for p in range(PIECES[ASIDE]):
+            sent_hop[p].wait_recv()
+            past_hop[p].start()
+
     smooth_depth(0)
-
-    for p in range(PIECES[ASIDE]):
-        sent_aside[p].wait_recv()
-    sent_tables[2].wait_recv()
-    take_table(ASIDE)
-    smooth_plane(ASIDE, lambda i: inv_smem[ASIDE][0, i])
 
     for slot, p, source, relay_at, target in RELAYED:
         @pl.when(place == relay_at)
@@ -286,19 +300,29 @@
             to_relay(slot, p, h_send.at[BEHIND, 0], beyond + source).wait_recv()
             from_relay(slot, p, here + target).start()
 
-    sent_far = halos(FAR, held[BEHIND], at(2))
+    onward = jnp.logical_and(inner, is_odd)
     for p in range(PIECES[BEHIND]):
         sent_behind[p].wait_recv()
 
-        @pl.when(inner)
+        @pl.when(onward)
         def _(p=p):
             sent_far[p].start()
 
-    sent_beside = halos(BESIDE, held[BEHIND], sibling)
     begin(sent_beside)
     sent_tables[0].wait_recv()
     take_table(BEHIND)
     smooth_plane(BEHIND, lambda i: inv_smem[BEHIND][0, i])
+
+    for p in range(PIECES[ASIDE]):
+        sent_aside[p].wait_recv()
+
+    @pl.when(is_odd)
+    def _():
+        begin(over_far)
+
+    sent_tables[2].wait_recv()
+    take_table(ASIDE)
+    smooth_plane(ASIDE, lambda i: inv_smem[ASIDE][0, i])
 
     smooth_depth(1)
 
@@ -336,7 +360,7 @@
     back = {}
     for i, slot in enumerate((BEHIND, BESIDE, FAR, ASIDE)):
         turned[i] = flipped[slot * ROWS : (slot + 1) * ROWS, :]
-    partners = (at(-2), at(-1 - 2 * odd), at(-4), at(1 + 2 * odd))
+    partners = (at(-2), at(-1 - 2 * odd), at(4 - 8 * odd), at(1 + 2 * odd))
     for i in range(4):
         back[i] = remote(turned.at[i], turned_in.at[i], b_send.at[i], b_recv.at[i], partners[i], c)
         back[i].start()
@@ -349,10 +373,9 @@
     def theirs(i):
         return turned_in[i][:, :ROWS]
 
-    is_odd = odd == 1
-    beside, aside = mine(BESIDE), mine(ASIDE)
+    beside, aside, far = mine(BESIDE), mine(ASIDE), mine(FAR)
     parts = [
-        mine(FAR),
+        jnp.where(is_odd, far, theirs(2)),
         jnp.where(is_odd, beside, theirs(3)),
         mine(BEHIND),
         jnp.where(is_odd, theirs(3), beside),
@@ -360,7 +383,7 @@
         jnp.where(is_odd, theirs(1), aside),
         theirs(0),
         jnp.where(is_odd, aside, theirs(1)),
-        theirs(2),
+        jnp.where(is_odd, theirs(2), far),
     ]
     whole = jnp.concatenate(parts, axis=1) * link[0:1, 0 : BAND * ROWS]
     for e in range(CELLS):
@@ -383,15 +406,25 @@
     for copy in (*sent_tables, *sent_behind, *sent_aside, *sent_beside, *back.values(), *given):
         copy.wait_send()
 
-    @pl.when(inner)
+    @pl.when(onward)
     def _():
         for copy in sent_far:
             copy.wait_send()
 
-    @pl.when(jnp.logical_or(place == 60, place == 61))
+    @pl.when(is_odd)
+    def _():
+        for copy in over_far:
+            copy.wait_send()
+
+    @pl.when(hops)
+    def _():
+        for copy in past_hop:
+            copy.wait_send()
+
+    @pl.when(place == 61)
     def _():
         for p in range(PIECES[FAR]):
-            halo(FAR, p, x_hbm, cross_send.at[p], beyond).wait_send()
+            halo(FAR, p, x_hbm, cross_send.at[p], beyond + 1).wait_send()
 
     for slot, p, source, relay_at, target in RELAYED:
         @pl.when(place == relay_at)
@@ -442,6 +475,7 @@
             dma((SLOTS, 4)), dma((SLOTS, 4)), dma((SLOTS,)), dma((SLOTS,)),
             dma((4,)), dma((4,)), dma((3,)), dma((3,)), dma((10,)),
             pltpu.VMEM((FOOT // 2, ROWS, WIDTH), BF16), dma((4,)), dma((1,)), dma((1,)),
+            pltpu.VMEM((FOOT, ROWS, WIDTH), BF16), dma((2,)), dma((2,)), dma((4,)),
         ],
         compiler_params=pltpu.CompilerParams(
             collective_id=0, has_side_effects=True, vmem_limit_bytes=56 * 2**20

time: 93.6 us -> 85.4 us (0.912)
  the two profiles are of different devices: /device:TPU:2 before, /device:TPU:62 now
where the time goes in v3:
time: 85.4 us; the launch traced here: 85.2 us
  Pallas kernels  80.6 us (94%)
  local copies, waits for them, and re-layouts  3.93 us (5%)
    pallas_call x1, Pallas kernels, body(): pl.pallas_call(kernel, out_shape=jax.ShapeDtypeStruct((ROWS, SHARE), F32)...  80.6 us
    unnamed x5, local copies, waits for them, and re-layouts  2.6 us

profile of v3, /device:TPU:62, one launch (start us, length us, event | category | flops | bytes accessed | tf_op | source)
XLA Modules:
  0.0 85.2 jit_solution(16115448166409235171)
XLA Ops:
  0.0 0.0 copy-start.1
  0.0 0.7 copy-done.1
  0.7 0.0 copy-start
  0.7 0.7 copy-done
  1.3 0.5 fusion.3.foot_own
  1.9 0.1 select_reduce_fusion
  2.0 0.6 broadcast_in_dim.27.inv_own.inv_vmem
  2.6 0.1 broadcast_in_dim.28
  2.7 0.7 broadcast_in_dim.29.link
  3.3 80.6 %band.1 = f32[16,36]{1,0:T(8,128)} custom-call(bf16[52,16,512]{2,1,0:T(8,128)(2,1)} %bitcast.4, s32[8,128]{1,0:T(8,128)} %broadcast_in_dim.27.inv_own.inv_vmem, s32[1,52]{1,0:T(1,128)} %fusion.3.foot_own, s32[8,128]{1,0:T(8,128)} %broadcast_in_dim.27.inv_own.inv_vmem, f32[1,144]{1,0:T(1,128)} %broadcast_in_dim.29.link, bf16[16,16]{1,0:T(8,128)(2,1)} %sx.1, ...), custom_call_target="tpu_custom_call" | custom-call | tf_op jit(solution)/shard_map/band/pallas_call | solution.py:449
  83.9 1.3 %copy.8 = f32[16,36]{1,0:T(8,128)} copy(f32[16,36]{1,0:T(8,128)} %band.1) | data formatting | bytes 4608
  (5 shorter events, 0.0 us)
Async XLA Ops:
  0.0 0.7 copy-start.1
  0.7 0.7 copy-start

commit v4 on v3

--- a/solution.py
+++ b/solution.py
@@ -20,25 +20,18 @@
 OWN, BEHIND, BESIDE, ASIDE, FAR = range(5)
 SLOTS = 5
 F32, BF16 = jnp.float32, jnp.bfloat16
-PIECES = {BEHIND: 4, BESIDE: 1, ASIDE: 2, FAR: 4}
+PIECES = {BEHIND: 8, BESIDE: 1, ASIDE: 8, FAR: 8}
+ROW_STAS = 8
 HALF_STAS = 64
 
 
-def crossings():
-    flows = []
-    for slot, source, column, target in ((BEHIND, 62, 0, 0), (BEHIND, 63, 1, 1), (FAR, 61, 3, 1)):
-        flows.append((slot, 0, source, None, target))
-        for p, row in enumerate((1, 7, 6), 1):
-            flows.append((slot, p, source, 8 * row + column, target))
-    for source, relay, target in ((0, 53, 61), (2, 52, 63)):
-        flows.append((ASIDE, 0, source, None, target))
-        flows.append((ASIDE, 1, source, relay, target))
-    return flows
-
-
-FLOWS = crossings()
-SOURCES = sorted({flow[2] for flow in FLOWS})
-RELAYED = [flow for flow in FLOWS if flow[3] is not None]
+CROSSINGS = (
+    (BEHIND, 62, 0, 0, 0), (BEHIND, 63, 1, 1, 0), (FAR, 61, 3, 1, 0), (ASIDE, 0, 2, 61, 7), (ASIDE, 2, 4, 63, 7)
+)
+
+
+def relay_rows(direct):
+    return [row for row in range(8) if row != direct]
 
 
 def iota(shape, dim):
@@ -95,18 +88,21 @@
         pl.semaphore_signal(barrier, inc=1, device_id=(at(distance), c), device_id_type=MESH)
     for j in (1, 2, 3):
         pl.semaphore_signal(barrier, inc=1, device_id=(s, lax.rem(c + j, CELLS)), device_id_type=MESH)
-    for slot, p, source, relay_at, target in RELAYED:
-        @pl.when(place == relay_at)
+    row, column = place // ROW_STAS, lax.rem(place, ROW_STAS)
+    relays = [jnp.logical_and(column == col, row != direct) for _, _, col, _, direct in CROSSINGS]
+    greeted = jnp.int32(11)
+    for acts, (slot, source, col, target, direct) in zip(relays, CROSSINGS):
+        greeted += jnp.where(acts, 1, 0) + jnp.where(place == source, 7, 0)
+
+        @pl.when(acts)
         def _(source=source):
             pl.semaphore_signal(barrier, inc=1, device_id=(beyond + source, c), device_id_type=MESH)
 
         @pl.when(place == target)
-        def _(relay_at=relay_at):
-            pl.semaphore_signal(barrier, inc=1, device_id=(here + relay_at, c), device_id_type=MESH)
-
-    greeted = jnp.int32(11)
-    for slot, p, source, relay_at, target in RELAYED:
-        greeted += jnp.where(jnp.logical_or(place == relay_at, place == source), 1, 0)
+        def _(col=col, direct=direct):
+            for r in relay_rows(direct):
+                pl.semaphore_signal(barrier, inc=1, device_id=(here + r * ROW_STAS + col, c), device_id_type=MESH)
+
     pl.semaphore_wait(barrier, greeted)
 
     def send_first(j, k):
@@ -129,9 +125,11 @@
         for j in (2, 1, 3):
             send_first(j, k).start()
 
+    def size_of(slot, p):
+        return FOOT if PIECES[slot] == 1 else 7 if p < 4 else 6
+
     def cut(slot, p):
-        size = FOOT // PIECES[slot]
-        return pl.ds(p * size, size)
+        return pl.ds(6 * p + min(p, 4), size_of(slot, p))
 
     def halo(slot, p, src, send, sta):
         return remote(src.at[cut(slot, p)], held[slot].at[cut(slot, p)], send, h_recv.at[slot, p], sta, c)
@@ -144,14 +142,30 @@
             copy.start()
 
     def to_relay(slot, p, send, sta):
-        size = FOOT // PIECES[slot]
-        return remote(x_hbm.at[cut(slot, p)], relay.at[pl.ds(0, size)], send, relay_recv.at[0], sta, c)
-
-    def from_relay(slot, p, sta):
-        size = FOOT // PIECES[slot]
-        return remote(
-            relay.at[pl.ds(0, size)], held[slot].at[cut(slot, p)], relay_send.at[0], h_recv.at[slot, p], sta, c
-        )
+        return remote(
+            x_hbm.at[cut(slot, p)], relay.at[pl.ds(0, size_of(slot, p))], send, relay_recv.at[0], sta, c
+        )
+
+    def from_relay(slot, p, size, start, sta):
+        return remote(
+            relay.at[pl.ds(0, size)], held[slot].at[pl.ds(start, size)],
+            relay_send.at[0], h_recv.at[slot, p], sta, c,
+        )
+
+    def relaying(begins):
+        for acts, (slot, source, col, target, direct) in zip(relays, CROSSINGS):
+            p = row if direct == 0 else row + 1
+            for size, fits in ((7, p < 4), (6, p >= 4)):
+                @pl.when(jnp.logical_and(acts, fits))
+                def _(slot=slot, source=source, target=target, p=p, size=size):
+                    start = 6 * p + (0 if size == 7 else 4)
+                    if size == 7:
+                        start = 7 * p
+                    if begins:
+                        to_relay(slot, 0 if size == 7 else 4, h_send.at[BEHIND, 0], beyond + source).wait_recv()
+                        from_relay(slot, p, size, start, here + target).start()
+                    else:
+                        from_relay(slot, p, size, start, here + target).wait_send()
 
     def table(slot, sta):
         return remote(inv_vmem, tables[slot], t_send.at[slot], t_recv.at[slot], sta, c)
@@ -187,16 +201,13 @@
     def _():
         begin(sent_hop)
 
-    for source_at in SOURCES:
-        @pl.when(place == source_at)
-        def _(source_at=source_at):
-            for slot, p, source, relay_at, target in FLOWS:
-                if source == source_at:
-                    send = cross_send.at[p] if slot == FAR else h_send.at[slot, p]
-                    if relay_at is None:
-                        halo(slot, p, x_hbm, send, beyond + target).start()
-                    else:
-                        to_relay(slot, p, send, beyond + relay_at).start()
+    for slot, source, col, target, direct in CROSSINGS:
+        @pl.when(place == source)
+        def _(slot=slot, col=col, target=target, direct=direct):
+            sends = [cross_send.at[p] if slot == FAR else h_send.at[slot, p] for p in range(8)]
+            for p, r in enumerate(relay_rows(direct), 1):
+                to_relay(slot, p, sends[p], beyond + r * ROW_STAS + col).start()
+            halo(slot, 0, x_hbm, sends[0], beyond + target).start()
 
     own_first = pltpu.make_async_copy(x_hbm.at[pl.ds(c * PART, PART)], first.at[c], local.at[0])
     own_first.start()
@@ -292,13 +303,9 @@
             sent_hop[p].wait_recv()
             past_hop[p].start()
 
+    relaying(True)
+
     smooth_depth(0)
-
-    for slot, p, source, relay_at, target in RELAYED:
-        @pl.when(place == relay_at)
-        def _(slot=slot, p=p, source=source, target=target):
-            to_relay(slot, p, h_send.at[BEHIND, 0], beyond + source).wait_recv()
-            from_relay(slot, p, here + target).start()
 
     onward = jnp.logical_and(inner, is_odd)
     for p in range(PIECES[BEHIND]):
@@ -426,10 +433,7 @@
         for p in range(PIECES[FAR]):
             halo(FAR, p, x_hbm, cross_send.at[p], beyond + 1).wait_send()
 
-    for slot, p, source, relay_at, target in RELAYED:
-        @pl.when(place == relay_at)
-        def _(slot=slot, p=p, target=target):
-            from_relay(slot, p, here + target).wait_send()
+    relaying(False)
 
 
 def body(sensitivity, footprint, linked, smooth_x, smooth_y, smooth_z):
@@ -472,10 +476,10 @@
             pltpu.VMEM((CELLS, ROWS, 128), F32),
             pltpu.VMEM((CELLS - 1, ROWS, 128), F32),
             dma((3, n_k)), dma((3, n_k)), dma((3, n_k)), dma((3, n_k)),
-            dma((SLOTS, 4)), dma((SLOTS, 4)), dma((SLOTS,)), dma((SLOTS,)),
+            dma((SLOTS, 8)), dma((SLOTS, 8)), dma((SLOTS,)), dma((SLOTS,)),
             dma((4,)), dma((4,)), dma((3,)), dma((3,)), dma((10,)),
-            pltpu.VMEM((FOOT // 2, ROWS, WIDTH), BF16), dma((4,)), dma((1,)), dma((1,)),
-            pltpu.VMEM((FOOT, ROWS, WIDTH), BF16), dma((2,)), dma((2,)), dma((4,)),
+            pltpu.VMEM((7, ROWS, WIDTH), BF16), dma((8,)), dma((1,)), dma((1,)),
+            pltpu.VMEM((FOOT, ROWS, WIDTH), BF16), dma((8,)), dma((8,)), dma((8,)),
         ],
         compiler_params=pltpu.CompilerParams(
             collective_id=0, has_side_effects=True, vmem_limit_bytes=56 * 2**20

time: 85.4 us -> 75.9 us (0.89)
  Pallas kernels: 80.6 us -> 71 us
    pallas_call x1, Pallas kernels: 80.6 us -> 71 us  [body(): pl.pallas_call(kernel, out_shape=jax.ShapeDtypeStruct((ROWS, SHARE), F32)...]
where the time goes in v4:
time: 75.9 us; the launch traced here: 75.6 us
  Pallas kernels  71 us (94%)
  local copies, waits for them, and re-layouts  3.93 us (5%)
    pallas_call x1, Pallas kernels, body(): pl.pallas_call(kernel, out_shape=jax.ShapeDtypeStruct((ROWS, SHARE), F32)...  71 us
    unnamed x5, local copies, waits for them, and re-layouts  2.6 us

profile of v4, /device:TPU:62, one launch (start us, length us, event | category | flops | bytes accessed | tf_op | source)
XLA Modules:
  0.0 75.6 jit_solution(8586204053995991732)
XLA Ops:
  0.0 0.0 copy-start.1
  0.0 0.7 copy-done.1
  0.7 0.0 copy-start
  0.7 0.7 copy-done
  1.3 0.5 fusion.3.foot_own
  1.9 0.1 select_reduce_fusion
  2.0 0.6 broadcast_in_dim.27.inv_own.inv_vmem
  2.6 0.1 broadcast_in_dim.28
  2.7 0.7 broadcast_in_dim.29.link
  3.3 71.0 %band.1 = f32[16,36]{1,0:T(8,128)} custom-call(bf16[52,16,512]{2,1,0:T(8,128)(2,1)} %bitcast.4, s32[8,128]{1,0:T(8,128)} %broadcast_in_dim.27.inv_own.inv_vmem, s32[1,52]{1,0:T(1,128)} %fusion.3.foot_own, s32[8,128]{1,0:T(8,128)} %broadcast_in_dim.27.inv_own.inv_vmem, f32[1,144]{1,0:T(1,128)} %broadcast_in_dim.29.link, bf16[16,16]{1,0:T(8,128)(2,1)} %sx.1, ...), custom_call_target="tpu_custom_call" | custom-call | tf_op jit(solution)/shard_map/band/pallas_call | solution.py:453
  74.3 1.3 %copy.8 = f32[16,36]{1,0:T(8,128)} copy(f32[16,36]{1,0:T(8,128)} %band.1) | data formatting | bytes 4608
  (5 shorter events, 0.0 us)
Async XLA Ops:
  0.0 0.7 copy-start.1
  0.7 0.7 copy-start

commit v5 on v4

--- a/solution.py
+++ b/solution.py
@@ -57,8 +57,8 @@
 
 
 def kernel(
-    x_hbm, inv_own, foot_own, inv_vmem, link, sx, sy, sz, out,
-    held, tables, inv_smem, first, second, smoothed, wz, kx, ky, wide_z, wide_x,
+    x_hbm, foot_own, linked, sx_hbm, sy_hbm, sz_hbm, out,
+    inv_own, inv_vmem, sx, sy, sz, held, tables, inv_smem, first, second, smoothed, wz, kx, ky, wide_z, wide_x,
     dense, across, field, square, turned, turned_in, shares, shares_in,
     z1_send, z1_recv, z2_send, z2_recv, h_send, h_recv, t_send, t_recv,
     b_send, b_recv, c_send, c_recv, local, relay, cross_send, relay_send, relay_recv,
@@ -83,6 +83,12 @@
     here = s - place
     beyond = HALF_STAS - here
 
+    fetched = [
+        pltpu.make_async_copy(src, dst, local.at[9 + i])
+        for i, (src, dst) in enumerate(((sx_hbm, sx), (sy_hbm, sy), (sz_hbm, sz)))
+    ]
+    for copy in fetched:
+        copy.start()
     barrier = pltpu.get_barrier_semaphore()
     for distance in (-4, -3, -2, -1, 1, 2, 3, 4):
         pl.semaphore_signal(barrier, inc=1, device_id=(at(distance), c), device_id_type=MESH)
@@ -102,6 +108,13 @@
         def _(col=col, direct=direct):
             for r in relay_rows(direct):
                 pl.semaphore_signal(barrier, inc=1, device_id=(here + r * ROW_STAS + col, c), device_id_type=MESH)
+
+    lanes = iota((8, 128), 1)
+    tile_at = lax.rem(lanes, 16) * 4 + lanes // 16
+    inverse = jnp.full((8, 128), FOOT, jnp.int32)
+    for f in range(FOOT):
+        inverse = jnp.where(tile_at == foot_own[0, f], f, inverse)
+    inv_vmem[...] = inverse
 
     pl.semaphore_wait(barrier, greeted)
 
@@ -211,11 +224,15 @@
 
     own_first = pltpu.make_async_copy(x_hbm.at[pl.ds(c * PART, PART)], first.at[c], local.at[0])
     own_first.start()
+    own_table = pltpu.make_async_copy(inv_vmem, inv_own, local.at[12])
+    own_table.start()
     own_held = pltpu.make_async_copy(x_hbm, held[OWN].at[pl.ds(0, FOOT)], local.at[1])
     own_held.start()
     for slot in range(SLOTS):
         held[slot][FOOT] = jnp.zeros((ROWS, WIDTH), BF16)
 
+    for copy in fetched:
+        copy.wait()
     kron_rows(sx, wide_x, kx)
     wide = iota((TILES, WIDTH), 1)
     spread = (iota((TILES, WIDTH), 0) == (wide // 128) * TILE + wide % TILE).astype(BF16)
@@ -255,6 +272,7 @@
         copy.wait()
 
     own_held.wait()
+    own_table.wait()
     smooth_plane(OWN, lambda i: inv_own[0, i])
 
     def send_second(j, k):
@@ -354,7 +372,7 @@
             for f in range(f0, f0 + fn):
                 place = e * PART + f
                 total = total + lax.dot_general(
-                    smoothed[place], field[foot_own[0, place]],
+                    smoothed[place], field[lax.rem(foot_own[0, place], 4) * 16 + foot_own[0, place] // 4],
                     (((1,), (1,)), ((), ())), preferred_element_type=F32,
                 )
             return total
@@ -392,7 +410,7 @@
         jnp.where(is_odd, aside, theirs(1)),
         jnp.where(is_odd, theirs(2), far),
     ]
-    whole = jnp.concatenate(parts, axis=1) * link[0:1, 0 : BAND * ROWS]
+    whole = jnp.concatenate([part * linked[0, j].astype(F32) for j, part in enumerate(parts)], axis=1)
     for e in range(CELLS):
         shares[e, :, 0:SHARE] = whole[:, e * SHARE : (e + 1) * SHARE]
     given = []
@@ -403,8 +421,8 @@
         given.append(copy)
     for copy in given:
         copy.wait_recv()
-    summed = shares[c] + shares_in[0] + shares_in[1] + shares_in[2]
-    out[...] = summed[:, 0:SHARE]
+    out[0] = shares[c] + shares_in[0]
+    out[1] = shares_in[1] + shares_in[2]
 
     for k in range(len(CHUNKS)):
         for j in (1, 2, 3):
@@ -438,24 +456,19 @@
 
 def body(sensitivity, footprint, linked, smooth_x, smooth_y, smooth_z):
     values = jnp.transpose(sensitivity, (1, 0, 2))
-    tiles = jnp.arange(TILES, dtype=jnp.int32)
-    tile_of = (tiles % 16) * 4 + tiles // 16
-    match = footprint[0][None, :] == tile_of[:, None]
-    order = jnp.arange(FOOT, dtype=jnp.int32)[None, :]
-    inverse = FOOT + jnp.sum(jnp.where(match, order - FOOT, 0), axis=1)
-    inverse = jnp.broadcast_to(jnp.pad(inverse, (0, 128 - TILES))[None, :], (8, 128))
-    foot = (footprint % 4) * 16 + footprint // 4
-    link = jnp.repeat(linked.astype(F32), ROWS, axis=1)
     n_k = len(CHUNKS)
     vmem = pl.BlockSpec(memory_space=pltpu.VMEM)
     smem = pl.BlockSpec(memory_space=pltpu.SMEM)
     dma = pltpu.SemaphoreType.DMA
-    return pl.pallas_call(
+    hbm = pl.BlockSpec(memory_space=pl.ANY)
+    shared = pl.pallas_call(
         kernel,
-        out_shape=jax.ShapeDtypeStruct((ROWS, SHARE), F32),
-        in_specs=[pl.BlockSpec(memory_space=pl.ANY), smem, smem, vmem, vmem, vmem, vmem, vmem],
+        out_shape=jax.ShapeDtypeStruct((2, ROWS, 128), F32),
+        in_specs=[hbm, smem, smem, hbm, hbm, hbm],
         out_specs=vmem,
         scratch_shapes=[
+            pltpu.SMEM((8, 128), jnp.int32), pltpu.VMEM((8, 128), jnp.int32),
+            pltpu.VMEM((16, 16), BF16), pltpu.VMEM((64, 64), BF16), pltpu.VMEM((128, 128), BF16),
             [pltpu.VMEM((FOOT + 1, ROWS, WIDTH), BF16)] * SLOTS,
             [pltpu.VMEM((8, 128), jnp.int32)] * SLOTS,
             [pltpu.SMEM((8, 128), jnp.int32)] * SLOTS,
@@ -477,7 +490,7 @@
             pltpu.VMEM((CELLS - 1, ROWS, 128), F32),
             dma((3, n_k)), dma((3, n_k)), dma((3, n_k)), dma((3, n_k)),
             dma((SLOTS, 8)), dma((SLOTS, 8)), dma((SLOTS,)), dma((SLOTS,)),
-            dma((4,)), dma((4,)), dma((3,)), dma((3,)), dma((10,)),
+            dma((4,)), dma((4,)), dma((3,)), dma((3,)), dma((13,)),
             pltpu.VMEM((7, ROWS, WIDTH), BF16), dma((8,)), dma((1,)), dma((1,)),
             pltpu.VMEM((FOOT, ROWS, WIDTH), BF16), dma((8,)), dma((8,)), dma((8,)),
         ],
@@ -485,7 +498,8 @@
             collective_id=0, has_side_effects=True, vmem_limit_bytes=56 * 2**20
         ),
         name="band",
-    )(values, inverse, foot, inverse, link, smooth_x, smooth_y, smooth_z)
+    )(values, footprint, linked, smooth_x, smooth_y, smooth_z)
+    return (shared[0] + shared[1])[:, :SHARE]
 
 
 def solution(mesh):

time: 75.9 us -> 72.4 us (0.954)
  local copies, waits for them, and re-layouts: 3.93 us -> 0 us
    unnamed x5 -> x0, local copies, waits for them, and re-layouts: 2.6 us -> none
    broadcast_in_dim x3 -> x0, local copies, waits for them, and re-layouts: 1.32 us -> none  [the longest x2 0.73 us: body(): link = jnp.repeat(linked.astype(F32), ROWS, axis=1)]
where the time goes in v5:
time: 72.4 us; the launch traced here: 72.3 us
  Pallas kernels  70.9 us (98%)
  other arithmetic  1.32 us (2%)
    pallas_call x1, Pallas kernels, body(): pl.pallas_call(kernel, out_shape=jax.ShapeDtypeStruct((2, ROWS, 128), F32...  70.9 us

profile of v5, /device:TPU:62, one launch (start us, length us, event | category | flops | bytes accessed | tf_op | source)
XLA Modules:
  0.0 72.3 jit_solution(14521896237915188075)
XLA Ops:
  0.0 70.9 %band.1 = f32[2,16,128]{2,1,0:T(8,128)} custom-call(bf16[52,16,512]{2,1,0:T(8,128)(2,1)} %bitcast.4, s32[1,52]{1,0:T(1,128)} %foot_own.1, s32[1,9]{1,0:T(1,128)} %linked.1, bf16[16,16]{1,0:T(8,128)(2,1)} %sx_hbm.1, bf16[64,64]{1,0:T(8,128)(2,1)} %sy_hbm.1, bf16[128,128]{1,0:T(8,128)(2,1)} %sz_hbm.1), custom_call_target="tpu_custom_call" | custom-call | tf_op jit(solution)/shard_map/band/pallas_call | solution.py:464
  70.9 1.3 %add_bitcast_fusion = f32[16,128]{1,0:T(8,128)} fusion(f32[2,16,128]{2,1,0:T(8,128)} %band.1), kind=kLoop, calls=%fused_computation | loop fusion | flops 2048 | bytes 24576 | tf_op jit(solution)/shard_map/add | solution.py:502

commit v6 on v5

--- a/solution.py
+++ b/solution.py
@@ -26,7 +26,7 @@
 
 
 CROSSINGS = (
-    (BEHIND, 62, 0, 0, 0), (BEHIND, 63, 1, 1, 0), (FAR, 61, 3, 1, 0), (ASIDE, 0, 2, 61, 7), (ASIDE, 2, 4, 63, 7)
+    (BEHIND, 62, 0, 0, 0), (BEHIND, 63, 1, 1, 0), (FAR, 61, 3, 1, 0), (ASIDE, 0, 4, 61, 7), (ASIDE, 2, 6, 63, 7)
 )
 
 
@@ -341,9 +341,9 @@
     for p in range(PIECES[ASIDE]):
         sent_aside[p].wait_recv()
 
-    @pl.when(is_odd)
-    def _():
-        begin(over_far)
+        @pl.when(is_odd)
+        def _(p=p):
+            over_far[p].start()
 
     sent_tables[2].wait_recv()
     take_table(ASIDE)

time: 72.4 us -> 71.8 us (level)
  no operation moved by 1% of the time
where the time goes in v6:
time: 71.8 us; the launch traced here: 71.7 us
  Pallas kernels  70.3 us (98%)
  other arithmetic  1.32 us (2%)
    pallas_call x1, Pallas kernels, body(): pl.pallas_call(kernel, out_shape=jax.ShapeDtypeStruct((2, ROWS, 128), F32...  70.3 us

profile of v6, /device:TPU:62, one launch (start us, length us, event | category | flops | bytes accessed | tf_op | source)
XLA Modules:
  0.0 71.7 jit_solution(3074486867059805003)
XLA Ops:
  0.0 70.3 %band.1 = f32[2,16,128]{2,1,0:T(8,128)} custom-call(bf16[52,16,512]{2,1,0:T(8,128)(2,1)} %bitcast.4, s32[1,52]{1,0:T(1,128)} %foot_own.1, s32[1,9]{1,0:T(1,128)} %linked.1, bf16[16,16]{1,0:T(8,128)(2,1)} %sx_hbm.1, bf16[64,64]{1,0:T(8,128)(2,1)} %sy_hbm.1, bf16[128,128]{1,0:T(8,128)(2,1)} %sz_hbm.1), custom_call_target="tpu_custom_call" | custom-call | tf_op jit(solution)/shard_map/band/pallas_call | solution.py:464
  70.3 1.3 %add_bitcast_fusion = f32[16,128]{1,0:T(8,128)} fusion(f32[2,16,128]{2,1,0:T(8,128)} %band.1), kind=kLoop, calls=%fused_computation | loop fusion | flops 2048 | bytes 24576 | tf_op jit(solution)/shard_map/add | solution.py:502

commit v7 on v6

--- a/solution.py
+++ b/solution.py
@@ -14,7 +14,7 @@
 CELLS = 4
 STAS = 128
 PART = FOOT // CELLS
-CHUNKS = ((0, 7), (7, 6))
+CHUNKS = ((0, 8), (8, 5))
 SHARE = BAND * ROWS // CELLS
 MESH = pl.DeviceIdType.MESH
 OWN, BEHIND, BESIDE, ASIDE, FAR = range(5)

time: 71.8 us -> 72.2 us (level)
  the two profiles are of different devices: /device:TPU:62 before, /device:TPU:2 now
where the time goes in v7:
time: 72.2 us; the launch traced here: 72.1 us
  Pallas kernels  70.7 us (98%)
  other arithmetic  1.32 us (2%)
    pallas_call x1, Pallas kernels, body(): pl.pallas_call(kernel, out_shape=jax.ShapeDtypeStruct((2, ROWS, 128), F32...  70.7 us

profile of v7, /device:TPU:2, one launch (start us, length us, event | category | flops | bytes accessed | tf_op | source)
XLA Modules:
  0.0 72.1 jit_solution(8607102567257585374)
XLA Ops:
  0.0 70.7 %band.1 = f32[2,16,128]{2,1,0:T(8,128)} custom-call(bf16[52,16,512]{2,1,0:T(8,128)(2,1)} %bitcast.4, s32[1,52]{1,0:T(1,128)} %foot_own.1, s32[1,9]{1,0:T(1,128)} %linked.1, bf16[16,16]{1,0:T(8,128)(2,1)} %sx_hbm.1, bf16[64,64]{1,0:T(8,128)(2,1)} %sy_hbm.1, bf16[128,128]{1,0:T(8,128)(2,1)} %sz_hbm.1), custom_call_target="tpu_custom_call" | custom-call | tf_op jit(solution)/shard_map/band/pallas_call | solution.py:464
  70.7 1.3 %add_bitcast_fusion = f32[16,128]{1,0:T(8,128)} fusion(f32[2,16,128]{2,1,0:T(8,128)} %band.1), kind=kLoop, calls=%fused_computation | loop fusion | flops 2048 | bytes 24576 | tf_op jit(solution)/shard_map/add | solution.py:502
